TPU v7x, 128 devices: a whole 4x4x4 slice. The times are simulated.
128 devices in a mesh: seq: 16 (over x_hi, y, core), grp: 8 (over x_lo, z).
Axes of the slice: x: 4 (x_hi: 2, x_lo: 2; x = x_hi * 2 + x_lo), y: 4, z: 4, core: 2. Of those that a mesh axis runs over, the one named last changes fastest.
Arguments:
- tokens: bfloat16 [1024, 32, 2048], P('grp', 'seq'), may hold values from -6 to 6
- norm_gain: float32 [2048], replicated, may hold values from 0.25 to 1.75
- qk_gain: float32 [2, 2, 16, 128], P(None, None, 'grp'), may hold values from 0.5 to 12
- window_blocks: int32 [8, 4], replicated, may hold values from 0 to 7, as said below
- w_spatial: bfloat16 [2048, 3, 2048], P('seq', None, 'grp'), may hold values from -0.13258252 to 0.13258252
- w_temporal: bfloat16 [2048, 3, 2048], P('seq', None, 'grp'), may hold values from -0.13258252 to 0.13258252
- w_out: bfloat16 [2048, 2, 2048], P('seq', None, 'grp'), may hold values from -0.09375 to 0.09375
Outputs:
- block_out: bfloat16 [1024, 32, 2048], P('grp', 'seq')
Inputs may be any that keep to these rules, and one draw needn't show every extreme that they name: `window_blocks`: row t lists 4 distinct tiles, the first of them t itself.
All inputs are finite; a program needn't handle non-finite values.
Results may differ from a plain program's by a relative error of at most 0.015.
Values may be sent and summed in bfloat16 or wider, within the bound.
A program may use at most 128 MiB of HBM per device.

v0:
```python
import jax
import jax.numpy as jnp
from jax import lax
from jax.sharding import PartitionSpec as P

TILE = 128


def rms_scale(values):
    return values * lax.rsqrt(jnp.mean(values * values, axis=-1, keepdims=True) + 1e-06)


def finish_heads(projected, gain_pair, head_count):
    head_width = gain_pair.shape[-1]
    shaped = projected.reshape(projected.shape[0], projected.shape[1], 3, head_count, head_width)
    queries = (rms_scale(shaped[:, :, 0]) * gain_pair[0] * head_width ** (-0.5)).astype(
        jnp.bfloat16
    )
    key_rows = (rms_scale(shaped[:, :, 1]) * gain_pair[1]).astype(jnp.bfloat16)
    values = shaped[:, :, 2].astype(jnp.bfloat16)
    return (queries, key_rows, values)


def spatial_attention(queries, key_rows, values, window_blocks, tile_rows):
    row_total, frames, head_count, head_width = queries.shape
    tile_count = row_total // tile_rows
    listed = window_blocks.shape[1]
    query_tiles = queries.reshape(tile_count, tile_rows, frames, head_count, head_width)
    key_tiles = key_rows.reshape(tile_count, tile_rows, frames, head_count, head_width)[
        window_blocks
    ]
    key_tiles = key_tiles.reshape(tile_count, listed * tile_rows, frames, head_count, head_width)
    value_tiles = values.reshape(tile_count, tile_rows, frames, head_count, head_width)[
        window_blocks
    ]
    value_tiles = value_tiles.reshape(
        tile_count, listed * tile_rows, frames, head_count, head_width
    )
    scores = jnp.einsum(
        "tqfhe,tkfhe->tfhqk", query_tiles, key_tiles, preferred_element_type=jnp.float32
    )
    scores = jnp.exp(scores - jnp.max(scores, axis=-1, keepdims=True))
    attn_weights = (scores / jnp.sum(scores, axis=-1, keepdims=True)).astype(jnp.bfloat16)
    attended = jnp.einsum(
        "tfhqk,tkfhe->tqfhe", attn_weights, value_tiles, preferred_element_type=jnp.float32
    )
    return attended.astype(jnp.bfloat16).reshape(row_total, frames, head_count, head_width)


def temporal_attention(queries, key_rows, values):
    frames = queries.shape[1]
    scores = jnp.einsum("rfhe,rghe->rhfg", queries, key_rows, preferred_element_type=jnp.float32)
    causal = lax.broadcasted_iota(jnp.int32, (frames, frames), 1) <= lax.broadcasted_iota(
        jnp.int32, (frames, frames), 0
    )
    scores = jnp.where(causal, scores, jnp.float32(-1e30))
    scores = jnp.exp(scores - jnp.max(scores, axis=-1, keepdims=True))
    attn_weights = (scores / jnp.sum(scores, axis=-1, keepdims=True)).astype(jnp.bfloat16)
    attended = jnp.einsum(
        "rhfg,rghe->rfhe", attn_weights, values, preferred_element_type=jnp.float32
    )
    return attended.astype(jnp.bfloat16)


def body(tokens, norm_gain, qk_gain, window_blocks, w_spatial, w_temporal, w_out):
    local_rows, frames_here, model_width = tokens.shape
    head_count = qk_gain.shape[2]
    head_width = qk_gain.shape[3]
    normed = (rms_scale(tokens.astype(jnp.float32)) * norm_gain).astype(jnp.bfloat16)
    gathered = lax.all_gather(normed, "grp", axis=0, tiled=True)
    row_total = gathered.shape[0]
    flattened = gathered.reshape(row_total * frames_here, model_width)
    column_count = w_spatial.shape[1] * w_spatial.shape[2]
    full_spatial, full_temporal, full_out = (
        lax.all_gather(w_spatial, "seq", axis=0, tiled=True),
        lax.all_gather(w_temporal, "seq", axis=0, tiled=True),
        lax.all_gather(w_out, "seq", axis=0, tiled=True),
    )
    spatial_proj = jnp.dot(
        flattened,
        full_spatial.reshape(model_width, column_count),
        preferred_element_type=jnp.float32,
    )
    temporal_proj = jnp.dot(
        flattened,
        full_temporal.reshape(model_width, column_count),
        preferred_element_type=jnp.float32,
    )
    spatial_q, spatial_k, spatial_v = finish_heads(
        spatial_proj.reshape(row_total, frames_here, column_count), qk_gain[0], head_count
    )
    temporal_q, temporal_k, temporal_v = finish_heads(
        temporal_proj.reshape(row_total, frames_here, column_count), qk_gain[1], head_count
    )
    packed = jnp.concatenate([temporal_q, temporal_k, temporal_v], axis=3)
    exchanged = lax.all_to_all(packed, "seq", split_axis=0, concat_axis=1, tiled=True)
    width_each = exchanged.shape[3] // 3
    attended = temporal_attention(
        exchanged[..., :width_each],
        exchanged[..., width_each : 2 * width_each],
        exchanged[..., 2 * width_each :],
    )
    temporal_out = lax.all_to_all(attended, "seq", split_axis=1, concat_axis=0, tiled=True)
    spatial_out = spatial_attention(spatial_q, spatial_k, spatial_v, window_blocks, TILE)
    branch_out = jnp.stack([spatial_out, temporal_out], axis=2).reshape(
        row_total, frames_here, 2, head_count * head_width
    )
    summed = lax.psum_scatter(
        jnp.einsum(
            "pfbc,dbc->pfd", branch_out, full_out, preferred_element_type=jnp.float32
        ).astype(jnp.bfloat16),
        "grp",
        scatter_dimension=0,
        tiled=True,
    ).astype(jnp.float32)
    return (tokens.astype(jnp.float32) + summed).astype(jnp.bfloat16)


def solution(mesh):
    return jax.shard_map(
        body,
        mesh=mesh,
        in_specs=(
            P("grp", "seq", None),
            P(),
            P(None, None, "grp", None),
            P(),
            P("seq", None, "grp"),
            P("seq", None, "grp"),
            P("seq", None, "grp"),
        ),
        out_specs=P("grp", "seq", None),
        check_vma=False,
    )
```

profile of v0, /device:TPU:1, one launch (start us, length us, event | category | flops | bytes accessed | tf_op | source)
XLA Modules:
  0.0 425.5 jit_solution(17707374089172688793)
XLA Ops:
  6.5 0.0 all-gather.9.cloned.1.call-start
  6.6 1.8 copy.73
  8.4 0.0 all-gather.9.cloned.1.call-update
  8.4 0.0 all-gather.5.cloned.1.call-start
  8.5 1.6 fusion.10
  10.1 2.8 fusion.12
  12.9 0.0 all-gather.5.cloned.1.call-update
  12.9 0.0 all-gather.7.cloned.1.call-start
  12.9 0.0 copy-done.4
  12.9 0.8 copy.61
  13.8 0.0 all-gather.7.cloned.1.call-update
  13.8 0.0 all-gather.11.cloned.1.call-start
  13.8 0.0 copy-done.5
  13.8 0.7 copy.83
  14.5 0.0 all-gather.11.cloned.1.call-update
  14.6 0.0 copy-done.6
  14.6 0.0 copy-done.7
  14.6 0.1 copy.62
  14.7 0.1 reshape.110
  14.8 50.2 %all-gather.9.cloned.1.call-done = bf16[2048,3,256]{0,2,1:T(8,128)(2,1)} async-done(((bf16[128,3,256]{0,2,1:T(8,128)(2,1)}), bf16[2048,3,256]{0,2,1:T(8,128)(2,1)}) %all-gather.9.cloned.1.call-update) | async-done | bytes 3145744 | tf_op jit(solution)/shard_map/all_gather | solution.py:76
  65.0 91.2 %all-gather.5.cloned.1.call-done = bf16[1024,2,2048]{2,0,1:T(8,128)(2,1)} async-done(((bf16[128,2,2048]{2,0,1:T(8,128)(2,1)}), bf16[1024,2,2048]{2,0,1:T(8,128)(2,1)}) %all-gather.5.cloned.1.call-update) | async-done | bytes 8388624 | tf_op jit(solution)/shard_map/all_gather | solution.py:70
  156.2 10.1 %fusion.2 = f32[1024,2,3,2,128]{0,4,3,2,1:T(8,128)S(1)} fusion(bf16[3,2,128,2048,1]{3,2,1,0,4:T(8,128)(2,1)} %bitcast.102, bf16[1024,2,2048]{2,0,1:T(8,128)(2,1)} %all-gather.5.cloned.1.call-done), kind=kOutput, calls=%fused_computation.5 | convolution fusion | flops 6442450944 | bytes 17825792 | tf_op jit(solution)/shard_map/dot_general | solution.py:84
  166.3 0.2 fusion.32
  166.4 0.6 multiply_reduce_fusion.1
  167.0 0.6 multiply_convert_fusion.1
  167.6 0.3 pad_maximum_fusion
  167.9 5.9 %copy.76 = bf16[1024,2,2,384]{3,2,1,0:T(2,128)(2,1)} copy(bf16[1024,2,2,384]{0,3,2,1:T(8,128)(2,1)S(1)} %pad_maximum_fusion) | data formatting | bytes 6291456 | tf_op jit(solution)/shard_map/concatenate | solution.py:95
  173.8 7.1 %all-to-all-start = ((bf16[1024,2,2,384]{3,2,1,0:T(2,128)(2,1)}), bf16[1024,2,2,384]{3,2,1,0:T(2,128)(2,1)}, u32[]{:S(2)}, u32[]{:S(2)}) async-start(bf16[1024,2,2,384]{3,2,1,0:T(2,128)(2,1)} %copy.76), calls=%async_computation | async-start | bytes 6291456 | tf_op jit(solution)/shard_map/all_to_all | solution.py:96
  181.0 50.6 %all-gather.7.cloned.1.call-done = bf16[2048,3,256]{0,2,1:T(8,128)(2,1)} async-done(((bf16[128,3,256]{0,2,1:T(8,128)(2,1)}), bf16[2048,3,256]{0,2,1:T(8,128)(2,1)}) %all-gather.7.cloned.1.call-update) | async-done | bytes 3145744 | tf_op jit(solution)/shard_map/all_gather | solution.py:75
  231.5 10.1 %fusion.4 = f32[1024,2,3,2,128]{4,0,3,2,1:T(8,128)S(1)} fusion(bf16[3,2,128,2048,1]{3,2,1,0,4:T(8,128)(2,1)} %bitcast.101, bf16[1024,2,2048]{2,0,1:T(8,128)(2,1)} %all-gather.5.cloned.1.call-done), kind=kOutput, calls=%fused_computation.7 | convolution fusion | flops 6442450944 | bytes 17825792 | tf_op jit(solution)/shard_map/dot_general | solution.py:79
  241.6 1.1 slice.115
  242.7 1.2 multiply_reduce_fusion.3
  243.9 0.0 copy-start.1
  244.0 0.9 fusion.19
  244.9 3.0 gather_fusion.1
  247.9 4.8 %copy.69 = bf16[32,128,2,2,128]{4,1,0,3,2:T(8,128)(2,1)} copy(bf16[32,128,2,2,128]{4,1,3,2,0:T(8,128)(2,1)} %gather_fusion.1) | data formatting | bytes 8388608 | tf_op jit(solution)/shard_map/gather | solution.py:29
  252.8 0.1 copy.63
  252.9 3.0 gather_fusion
  255.9 4.7 %copy.64 = bf16[32,128,2,2,128]{4,1,0,3,2:T(8,128)(2,1)} copy(bf16[32,128,2,2,128]{4,1,3,2,0:T(8,128)(2,1)} %gather_fusion) | data formatting | bytes 8388608 | tf_op jit(solution)/shard_map/gather | solution.py:33
  260.6 5.0 %fusion.70 = f32[8,2,2,128]{3,2,1,0:T(2,128)S(1)} fusion(bf16[8,512,2,2,128]{4,1,0,3,2:T(8,128)(2,1)} %bitcast.88, f32[8,128,2,2,128]{4,1,0,3,2:T(8,128)S(1)} %bitcast.92, f32[2,128]{1,0:T(2,128)S(1)} %get-tuple-element.13, f32[8,128,2,2]{1,3,2,0:T(2,128)S(1)} %bitcast.98), kind=kOutput, calls=%fused_computation.84 | convolution fusion | flops 543162880 | bytes 6325248 | tf_op jit(solution)/shard_map/sub | solution.py:42
  265.6 0.0 all-to-all-done
  265.6 2.3 copy.77
  267.9 3.2 copy.78
  271.2 2.7 all_to_all.27
  273.9 2.4 fusion.65
  276.3 1.8 fusion.30
  278.0 0.0 copy-start.2
  278.1 2.1 copy.80
  280.1 6.1 %all-to-all-start.1 = ((bf16[64,32,2,128]{3,2,0,1:T(2,128)(2,1)}), bf16[64,32,2,128]{3,2,0,1:T(2,128)(2,1)S(1)}, u32[]{:S(2)}, u32[]{:S(2)}) async-start(bf16[64,32,2,128]{3,2,0,1:T(2,128)(2,1)} %copy.80), calls=%async_computation.1 | async-start | bytes 2097152 | tf_op jit(solution)/shard_map/all_to_all | solution.py:103
  286.2 0.0 reduce-scatter.2.cloned.1.call-start
  286.3 0.0 copy-done.2
  286.3 7.7 %fusion.8 = f32[8,2,2,128,512]{4,3,2,1,0:T(8,128)} fusion(bf16[8,512,2,2,128]{4,1,0,3,2:T(8,128)(2,1)} %bitcast.89, f32[8,128,2,2,128]{4,1,0,3,2:T(8,128)S(1)} %bitcast.93, f32[2,128]{1,0:T(2,128)S(1)} %get-tuple-element.13, f32[8,128,2,2]{1,3,2,0:T(2,128)S(1)} %bitcast.99), kind=kOutput, calls=%fused_computation.13 | convolution fusion | flops 538968064 | bytes 14697472 | tf_op jit(solution)/shard_map/tqfhe,tkfhe->tfhqk/dot_general | solution.py:39
  294.0 15.5 %fusion.27 = bf16[8,128,2,2,128]{1,4,3,2,0:T(8,128)(2,1)S(1)} fusion(f32[8,2,2,128]{3,2,1,0:T(2,128)S(1)} %fusion.70, bf16[8,512,2,2,128]{4,1,0,3,2:T(8,128)(2,1)} %bitcast.94, f32[8,2,2,128,512]{4,3,2,1,0:T(8,128)} %fusion.8), kind=kOutput, calls=%fused_computation.50 | convolution fusion | flops 543691264 | bytes 13647872 | tf_op jit(solution)/shard_map/tfhqk,tkfhe->tqfhe/dot_general | solution.py:44
  309.5 0.8 copy.90
  310.3 0.7 reshape.135
  311.0 0.0 all-to-all-done.1
  311.0 1.2 copy.131
  312.3 0.7 stack.9
  313.0 0.0 all-gather.11.cloned.1.call-done
  313.0 8.3 %bitcast_convert_fusion = bf16[1024,2,2048]{2,0,1:T(8,128)(2,1)} fusion(bf16[1024,2,1,256]{3,0,2,1:T(8,128)(2,1)S(1)} %stack.9, bf16[1024,2,1,256]{3,0,2,1:T(8,128)(2,1)S(1)} %reshape.135, bf16[2048,2,256]{2,0,1:T(8,128)(2,1)} %all-gather.11.cloned.1.call-done), kind=kOutput, calls=%fused_computation.4 | convolution fusion | flops 4300210176 | bytes 12582912 | tf_op jit(solution)/shard_map/pfbc,dbc->pfd/dot_general | solution.py:109
  321.3 0.0 reduce-scatter.2.cloned.1.call-update
  321.4 93.9 %reduce-scatter.2.cloned.1.call-done = bf16[128,2,2048]{2,0,1:T(8,128)(2,1)} async-done(((bf16[1024,2,2048]{2,0,1:T(8,128)(2,1)}), bf16[128,2,2048]{2,0,1:T(8,128)(2,1)}) %reduce-scatter.2.cloned.1.call-update) | async-done | bytes 1048592 | tf_op jit(solution)/shard_map/reduce_scatter | solution.py:108
  415.3 1.7 fusion.13
  417.0 2.0 copy.84
  (18 shorter events, 0.1 us)
Async XLA Ops:
  6.5 6.4 %copy-start.4 = (bf16[128,3,256]{2,0,1:T(8,128)(2,1)S(1)}, bf16[128,3,256]{2,0,1:T(8,128)(2,1)}, u32[]{:S(2)}) copy-start(bf16[128,3,256]{2,0,1:T(8,128)(2,1)} %param.11) | copy-start | bytes 589828
  6.5 7.3 %copy-start.5 = (bf16[128,2,256]{2,1,0:T(2,128)(2,1)S(1)}, bf16[128,2,256]{2,1,0:T(2,128)(2,1)}, u32[]{:S(2)}) copy-start(bf16[128,2,256]{2,1,0:T(2,128)(2,1)} %param.13) | copy-start | bytes 393220
  6.5 8.0 %copy-start.6 = (f32[2,2,2,128]{3,2,1,0:T(2,128)S(1)}, f32[2,2,2,128]{3,2,1,0:T(2,128)}, u32[]{:S(2)}) copy-start(f32[2,2,2,128]{3,2,1,0:T(2,128)} %param.9) | copy-start | bytes 12292
  6.5 8.0 %copy-start.7 = (s32[8,4]{0,1:T(4,128)S(1)}, s32[8,4]{0,1:T(4,128)}, u32[]{:S(2)}) copy-start(s32[8,4]{0,1:T(4,128)} %param.10) | copy-start | bytes 388
  6.5 58.5 %all-gather.9.cloned.1.call-start = ((), (), s32[]{:S(2)}) async-start(), calls=%async_computation.5 | async-start | bytes 3342336 | tf_op jit(solution)/shard_map/all_gather | solution.py:76
  8.4 147.8 %all-gather.5.cloned.1.call-start = ((), (), s32[]{:S(2)}) async-start(), calls=%async_computation.3 | async-start | bytes 9437184 | tf_op jit(solution)/shard_map/all_gather | solution.py:70
  12.9 218.7 %all-gather.7.cloned.1.call-start = ((), (), s32[]{:S(2)}) async-start(), calls=%async_computation.4 | async-start | bytes 3342336 | tf_op jit(solution)/shard_map/all_gather | solution.py:75
  13.8 299.2 %all-gather.11.cloned.1.call-start = ((), (), s32[]{:S(2)}) async-start(), calls=%async_computation.6 | async-start | bytes 2228224 | tf_op jit(solution)/shard_map/all_gather | solution.py:77
  173.8 91.8 %all-to-all-start = ((bf16[1024,2,2,384]{3,2,1,0:T(2,128)(2,1)}), bf16[1024,2,2,384]{3,2,1,0:T(2,128)(2,1)}, u32[]{:S(2)}, u32[]{:S(2)}) async-start(bf16[1024,2,2,384]{3,2,1,0:T(2,128)(2,1)} %copy.76), calls=%async_computation | async-start | bytes 6291456 | tf_op jit(solution)/shard_map/all_to_all | solution.py:96
  243.9 16.7 %copy-start.1 = (f32[1024,2,1,2,128]{4,0,3,2,1:T(8,128)}, f32[1024,2,1,2,128]{4,0,3,2,1:T(8,128)S(1)}, u32[]{:S(2)}) copy-start(f32[1024,2,1,2,128]{4,0,3,2,1:T(8,128)S(1)} %get-tuple-element.9) | copy-start | bytes 6291460
  247.9 4.8 %copy-start.3 = (bf16[1024,2,1,2,128]{4,0,3,2,1:T(8,128)(2,1)S(1)}, bf16[1024,2,1,2,128]{4,0,3,2,1:T(8,128)(2,1)}, u32[]{:S(2)}) copy-start(bf16[1024,2,1,2,128]{4,0,3,2,1:T(8,128)(2,1)} %slice.115) | copy-start | bytes 3145732
  278.0 8.3 %copy-start.2 = (f32[1024,2,1,2,128]{4,0,3,2,1:T(8,128)S(1)}, f32[1024,2,1,2,128]{4,0,3,2,1:T(8,128)}, u32[]{:S(2)}) copy-start(f32[1024,2,1,2,128]{4,0,3,2,1:T(8,128)} %copy-done.1) | copy-start | bytes 6291460
  280.1 30.9 %all-to-all-start.1 = ((bf16[64,32,2,128]{3,2,0,1:T(2,128)(2,1)}), bf16[64,32,2,128]{3,2,0,1:T(2,128)(2,1)S(1)}, u32[]{:S(2)}, u32[]{:S(2)}) async-start(bf16[64,32,2,128]{3,2,0,1:T(2,128)(2,1)} %copy.80), calls=%async_computation.1 | async-start | bytes 2097152 | tf_op jit(solution)/shard_map/all_to_all | solution.py:103
  286.2 129.0 %reduce-scatter.2.cloned.1.call-start = ((), (), s32[]{:S(2)}) async-start(), calls=%async_computation.7 | async-start | bytes 9437184 | tf_op jit(solution)/shard_map/reduce_scatter | solution.py:108
  321.3 93.9 %copy-start = (bf16[128,2,2048]{2,1,0:T(2,128)(2,1)S(1)}, bf16[128,2,2048]{2,1,0:T(2,128)(2,1)}, u32[]{:S(2)}) copy-start(bf16[128,2,2048]{2,1,0:T(2,128)(2,1)} %param.7) | copy-start | bytes 3145732
Sparse Core Ops, SparseCore 0:
  9.6 55.3 all-gather.8
  66.7 89.4 all-gather.4
  158.5 73.0 all-gather.6
  233.9 47.5 all-gather.10
  321.5 93.7 reduce-scatter.1
where the time goes:
time: 426 us
  waiting for transfers between devices  286 us (67%)
  matrix products  60.8 us (14%)
  local copies, waits for them, and re-layouts  42.2 us (10%)
  starting transfers between devices  13.5 us (3%)
  between operations  13.4 us (3%)
  other arithmetic  9.69 us (2%)
    reduce_scatter x1, waiting for transfers between devices, body(): lax.psum_scatter(jnp.einsum('pfbc,dbc->pfd', branch_out, full_out, prefer...  93.9 us
    all_gather x1, waiting for transfers between devices, body(): gathered = lax.all_gather(normed, 'grp', axis=0, tiled=True)  91.2 us
    all_gather x1, waiting for transfers between devices, body(): lax.all_gather(w_spatial, 'seq', axis=0, tiled=True)  50.6 us
    all_gather x1, waiting for transfers between devices, body(): lax.all_gather(w_temporal, 'seq', axis=0, tiled=True)  50.2 us
    dot_general x1, matrix products, spatial_attention(): jnp.einsum('tfhqk,tkfhe->tqfhe', attn_weights, value_tiles, preferred_ele...  15.5 us
    dot_general x1, matrix products, body(): jnp.dot(flattened, full_spatial.reshape(model_width, column_count), prefe...  10.1 us
    dot_general x1, matrix products, body(): jnp.dot(flattened, full_temporal.reshape(model_width, column_count), pref...  10.1 us
  transfers between devices with their start and end apart: 7, of which 4 were waited for; matrix products, arithmetic and copies ran while one was open for 23% of the time, Pallas kernels for 0%

commit v1 on v0

v1 whole, which is shorter than its diff:
```python
import jax
import jax.numpy as jnp
from jax import lax
from jax.experimental import pallas as pl
from jax.experimental.pallas import tpu as pltpu
from jax.sharding import PartitionSpec as P

MESH = pl.DeviceIdType.MESH
EPS = 1e-06
F32 = jnp.float32
BF16 = jnp.bfloat16

TOK, WGT, OUTW, GAIN, RING_T, RING_W2, RING_WX, RING_O2, RING_OX, RS, FIN = (
    0, 4, 8, 10, 12, 18, 24, 30, 36, 42, 48,
)
SLOTS = 52


def mm(a, b):
    return jnp.dot(a, b, preferred_element_type=F32)


def mm_t(a, b):
    return lax.dot_general(a, b, (((1,), (1,)), ((), ())), preferred_element_type=F32)


def kernel(
    win, tok, norm_gain, gain, w_s, w_t, wo_s, wo_t, out,
    nrm, xs, wg, wo, gn, qkv, att, part, rs1, rs2, fin, snd, rcv,
):
    s, g = lax.axis_index("seq"), lax.axis_index("grp")
    c, y, xh = lax.rem(s, 2), lax.rem(lax.div(s, 2), 4), lax.div(s, 8)
    xl, z = lax.div(g, 4), lax.rem(g, 4)
    x = xh * 2 + xl
    nc = 1 - c
    unit = c * y + nc * z
    unit2 = nc * y + c * z

    def dev(xh_, y_, c_, xl_, z_):
        return ((xh_ * 4 + y_) * 2 + c_, xl_ * 4 + z_)

    def remote(src, dst, i, j, to):
        return pltpu.make_async_remote_copy(
            src_ref=src, dst_ref=dst, send_sem=snd.at[i], recv_sem=rcv.at[j],
            device_id=to, device_id_type=MESH,
        )

    sends = []

    def put(src, dst, i, j, to):
        mine = jnp.logical_and(to[0] == s, to[1] == g)
        copy = remote(src, dst, i, j, to)

        @pl.when(mine)
        def _():
            pltpu.make_async_copy(src, dst, rcv.at[j]).start()

        @pl.when(jnp.logical_not(mine))
        def _():
            copy.start()

        sends.append((copy, jnp.logical_not(mine)))

    def arrived(dst, j):
        pltpu.make_async_copy(dst, dst, rcv.at[j]).wait()

    def start(copy):
        copy.start()
        sends.append((copy, None))

    class Ring:
        def __init__(self, view, at, right, left, base):
            self.view, self.at, self.base = view, at, base
            self.right, self.left = right, left
            self.units = (at, lax.rem(at + 3, 4), lax.rem(at + 1, 4), lax.rem(at + 2, 4))

        def send(self, u, half, k, to):
            ref = self.view(self.units[u], half)
            start(remote(ref, ref, self.base + k, self.base + k, to))

        def begin(self):
            self.send(0, 0, 0, self.right)
            self.send(0, 1, 3, self.left)
            self.send(0, 1, 1, self.right)
            self.send(0, 0, 4, self.left)

        def forward(self):
            arrived(self.view(self.units[1], 0), self.base + 0)
            self.send(1, 0, 2, self.right)
            arrived(self.view(self.units[2], 1), self.base + 3)
            self.send(2, 1, 5, self.left)

        def near(self):
            arrived(self.view(self.units[1], 1), self.base + 1)
            arrived(self.view(self.units[2], 0), self.base + 4)

        def far(self):
            arrived(self.view(self.units[3], 0), self.base + 2)
            arrived(self.view(self.units[3], 1), self.base + 5)

    def along(dy, dz):
        return dev(xh, lax.rem(y + dy, 4), c, xl, lax.rem(z + dz, 4))

    def across(dx):
        nx = lax.rem(x + dx, 4)
        return dev(lax.div(nx, 2), y, c, lax.rem(nx, 2), z)

    right, left = along(c, nc), along(3 * c, 3 * nc)
    right2, left2 = along(nc, c), along(3 * nc, 3 * c)

    ring_t = Ring(lambda u, h: xs.at[u, pl.ds(h * 256, 256)], unit, right, left, RING_T)
    ring_w2 = Ring(
        lambda u, h: wg.at[x, pl.ds(u * 256 + h * 128, 128)], unit2, right2, left2, RING_W2
    )
    ring_wx = Ring(
        lambda u, h: wg.at[u, pl.ds(h * 512, 512)], x, across(1), across(3), RING_WX
    )
    ring_o2 = Ring(
        lambda u, h: wo.at[x, pl.ds(u * 256 + h * 128, 128)], unit2, right2, left2, RING_O2
    )
    ring_ox = Ring(
        lambda u, h: wo.at[u, pl.ds(h * 512, 512)], x, across(1), across(3), RING_OX
    )

    to_s, to_t = dev(xh, y, 0, xl, z), dev(xh, z, 1, xl, y)
    row_s = y * 256 + c * 128
    put(w_s, wg.at[x, pl.ds(row_s, 128)], WGT, WGT + c, to_s)
    put(w_t, wg.at[x, pl.ds(row_s, 128)], WGT + 1, WGT + c, to_t)

    for h in range(2):
        def norm_rows(k, _):
            rows = pl.ds(pl.multiple_of(h * 128 + k * 32, 32), 32)
            v = tok[rows, :].astype(F32)
            scale = lax.rsqrt(jnp.mean(v * v, axis=-1, keepdims=True) + EPS)
            nrm[rows, :] = (v * scale * norm_gain[...]).astype(BF16)
            return 0

        lax.fori_loop(0, 4, norm_rows, 0)
        src = nrm.at[pl.ds(h * 128, 128)]
        i_s, i_t = xl * 2 + h, xh * 2 + c
        put(src, xs.at[z, pl.ds(i_s * 128, 128)], TOK + h, TOK + i_s, dev(xh, y, 0, c, z))
        put(src, xs.at[y, pl.ds(i_t * 128, 128)], TOK + 2 + h, TOK + i_t, dev(h, y, 1, xl, z))

    put(wo_s, wo.at[x, pl.ds(row_s, 128)], OUTW, OUTW + c, to_s)
    put(wo_t, wo.at[x, pl.ds(row_s, 128)], OUTW + 1, OUTW + c, to_t)
    for h in range(2):
        put(
            gain.at[c], gn.at[xl], GAIN + h, GAIN + xl,
            dev(xh, nc * y + c * z, c, h, nc * z + c * y),
        )

    for i in range(2):
        arrived(wg.at[x, pl.ds(unit2 * 256 + i * 128, 128)], WGT + i)
    ring_w2.begin()
    for i in range(4):
        arrived(xs.at[unit, pl.ds(i * 128, 128)], TOK + i)
    ring_t.begin()
    ring_w2.forward()
    ring_w2.near()
    ring_w2.far()
    ring_wx.begin()
    for i in range(2):
        arrived(wo.at[x, pl.ds(unit2 * 256 + i * 128, 128)], OUTW + i)
        arrived(gn.at[i], GAIN + i)
    ring_o2.begin()
    ring_t.forward()
    ring_o2.forward()
    ring_o2.near()
    ring_o2.far()
    ring_wx.forward()
    ring_ox.begin()
    ring_t.near()
    ring_t.far()
    ring_wx.near()

    def project(pair):
        def one(u, _):
            for n in range(3):
                cols = slice(n * 256, n * 256 + 256)
                acc = mm(xs[u, :, 0:1024], wg[pair, :, cols])
                acc = acc + mm(xs[u, :, 1024:2048], wg[2 + pair, :, cols])
                for j in range(2):
                    a = acc[:, j * 128 : j * 128 + 128]
                    if n < 2:
                        a = a * lax.rsqrt(jnp.mean(a * a, axis=-1, keepdims=True) + EPS)
                        a = a * gn[pair, 2 * n + j : 2 * n + j + 1, :]
                    if n == 0:
                        a = a * (128 ** -0.5)
                    a = a.astype(BF16)
                    for k in range(8):
                        i, f = k // 2, k % 2
                        t = (i // 2) * 4 + u
                        to_row = nc * (f * 16 + t * 2 + i % 2) + c * (t * 4 + i % 2 * 2 + f)
                        qkv[n, pair * 2 + j, to_row] = a[k * 64 : k * 64 + 64]
            return 0

        lax.fori_loop(0, 4, one, 0)

    project(1 - xl)
    ring_ox.forward()
    ring_wx.far()
    project(xl)
    ring_ox.near()
    ring_ox.far()

    @pl.when(c == 0)
    def _():
        def spatial(ft, _):
            f, t = lax.div(ft, 8), lax.rem(ft, 8)
            at = [f * 16 + 2 * win[t, j] for j in range(4)]
            for hd in range(4):
                q = qkv[0, hd, pl.ds(f * 16 + 2 * t, 2)].reshape(128, 128)
                sc = [mm_t(q, qkv[1, hd, pl.ds(a, 2)].reshape(128, 128)) for a in at]
                top = jnp.maximum(jnp.maximum(sc[0], sc[1]), jnp.maximum(sc[2], sc[3]))
                top = jnp.max(top, axis=-1, keepdims=True)
                sc = [jnp.exp(v - top) for v in sc]
                total = jnp.sum(sc[0] + sc[1] + sc[2] + sc[3], axis=-1, keepdims=True)
                inv = 1.0 / total
                o = 0.0
                for v, a in zip(sc, at):
                    o = o + mm((v * inv).astype(BF16), qkv[2, hd, pl.ds(a, 2)].reshape(128, 128))
                o = o.astype(BF16)
                for h in range(2):
                    att[
                        lax.rem(t, 4), lax.div(t, 4) * 4 + h * 2 + f, :, hd * 128 : hd * 128 + 128
                    ] = o[h * 64 : h * 64 + 64]
            return 0

        lax.fori_loop(0, 16, spatial, 0)

    @pl.when(c == 1)
    def _():
        def temporal(pg, _):
            rows = pl.ds(pl.multiple_of(pg * 16, 16), 16)
            for hd in range(4):
                q, k, v = (qkv[n, hd, :, rows, :].reshape(512, 128) for n in range(3))
                for b in range(2):
                    keys = 256 * (b + 1)
                    sc = mm_t(q[b * 256 : b * 256 + 256], k[:keys])
                    qi = lax.broadcasted_iota(jnp.int32, (256, keys), 0) + b * 256
                    ki = lax.broadcasted_iota(jnp.int32, (256, keys), 1)
                    ok = jnp.logical_and(
                        jnp.bitwise_and(qi, 15) == jnp.bitwise_and(ki, 15), ki <= qi
                    )
                    sc = jnp.where(ok, sc, -1e30)
                    sc = jnp.exp(sc - jnp.max(sc, axis=-1, keepdims=True))
                    inv = 1.0 / jnp.sum(sc, axis=-1, keepdims=True)
                    o = mm((sc * inv).astype(BF16), v[:keys]).astype(BF16)
                    for m in range(16):
                        fr = b * 16 + m
                        t = fr // 4
                        i = (t // 4) * 2 + (fr // 2) % 2
                        att[t % 4, i * 2 + fr % 2, rows, hd * 128 : hd * 128 + 128] = o[
                            m * 16 : m * 16 + 16
                        ]
            return 0

        lax.fori_loop(0, 4, temporal, 0)

    def outproj(u):
        def one(k, _):
            o = att[u].reshape(512, 512)
            half, rows = lax.div(k, 4), pl.ds(pl.multiple_of(lax.rem(k, 4) * 256, 256), 256)
            acc = mm_t(o[:, 0:256], wo[half * 2, rows, :])
            acc = acc + mm_t(o[:, 256:512], wo[half * 2 + 1, rows, :])
            part[u, :, pl.ds(pl.multiple_of(k * 256, 256), 256)] = acc.astype(BF16)
            return 0

        lax.fori_loop(0, 8, one, 0)

    def add_rows(u, first, count, others):
        def one(k, _):
            rows = pl.ds(pl.multiple_of(first + k * 32, 32), 32)
            total = part[u, rows, :].astype(F32)
            for other, off in others:
                at = pl.ds(pl.multiple_of(first - off + k * 32, 32), 32)
                total = total + other[at, :].astype(F32)
            part[u, rows, :] = total.astype(BF16)
            return 0

        lax.fori_loop(0, count // 32, one, 0)

    A, B = pl.ds(0, 256), pl.ds(256, 256)
    u_l, u_r, u_2 = lax.rem(unit + 3, 4), lax.rem(unit + 1, 4), lax.rem(unit + 2, 4)
    outproj(u_2)
    start(remote(part.at[u_2, A], rs1.at[0], RS, RS, right))
    start(remote(part.at[u_2, B], rs1.at[1], RS + 1, RS + 1, left))
    outproj(u_r)
    start(remote(part.at[u_r, B], rs2.at[0, B], RS + 2, RS + 2, right))
    outproj(u_l)
    start(remote(part.at[u_l, A], rs2.at[1, A], RS + 3, RS + 3, left))
    arrived(rs1.at[0], RS)
    add_rows(u_r, 0, 256, [(rs1.at[0], 0)])
    start(remote(part.at[u_r, A], rs2.at[0, A], RS + 4, RS + 4, right))
    arrived(rs1.at[1], RS + 1)
    add_rows(u_l, 256, 256, [(rs1.at[1], 256)])
    start(remote(part.at[u_l, B], rs2.at[1, B], RS + 5, RS + 5, left))
    outproj(unit)

    def finish(i):
        a, b = i // 2, i % 2
        slot = nc * b + c * (2 + xh)
        to = dev(nc * xh + c * a, y, nc * xl + c * b, nc * a + c * xl, z)
        put(part.at[unit, pl.ds(i * 128, 128)], fin.at[slot], FIN + i, FIN + slot, to)

    arrived(rs2.at[0, B], RS + 2)
    arrived(rs2.at[1, A], RS + 3)
    arrived(rs2.at[0, A], RS + 4)
    add_rows(unit, 0, 256, [(rs2.at[0], 0), (rs2.at[1], 0)])
    finish(0)
    finish(1)
    arrived(rs2.at[1, B], RS + 5)
    add_rows(unit, 256, 256, [(rs2.at[0], 0), (rs2.at[1], 0)])
    finish(2)
    finish(3)

    for h in range(2):
        arrived(fin.at[h], FIN + h)
        arrived(fin.at[2 + h], FIN + 2 + h)

        def total_rows(k, _):
            rows = pl.ds(pl.multiple_of(k * 32, 32), 32)
            here = pl.ds(pl.multiple_of(h * 128 + k * 32, 32), 32)
            total = fin[h, rows, :].astype(F32) + fin[2 + h, rows, :].astype(F32)
            out[here, :] = (tok[here, :].astype(F32) + total).astype(BF16)
            return 0

        lax.fori_loop(0, 4, total_rows, 0)

    for copy, cond in sends:
        if cond is None:
            copy.wait_send()
        else:
            pl.when(cond)(copy.wait_send)


def body(tokens, norm_gain, qk_gain, window_blocks, w_spatial, w_temporal, w_out):
    rows, frames, width = tokens.shape
    tok = tokens.reshape(2, 64, 2, width).transpose(0, 2, 1, 3).reshape(256, width)
    vmem = pl.BlockSpec(memory_space=pltpu.VMEM)
    res = pl.pallas_call(
        kernel,
        name="attention_block",
        out_shape=jax.ShapeDtypeStruct((256, width), BF16),
        in_specs=[pl.BlockSpec(memory_space=pltpu.SMEM)] + [vmem] * 7,
        out_specs=vmem,
        scratch_shapes=[
            pltpu.VMEM((256, 2048), BF16),
            pltpu.VMEM((4, 512, 2048), BF16),
            pltpu.VMEM((4, 1024, 768), BF16),
            pltpu.VMEM((4, 1024, 256), BF16),
            pltpu.VMEM((2, 4, 128), F32),
            pltpu.VMEM((3, 4, 32, 64, 128), BF16),
            pltpu.VMEM((4, 8, 64, 512), BF16),
            pltpu.VMEM((4, 512, 2048), BF16),
            pltpu.VMEM((2, 256, 2048), BF16),
            pltpu.VMEM((2, 512, 2048), BF16),
            pltpu.VMEM((4, 128, 2048), BF16),
            pltpu.SemaphoreType.DMA((SLOTS,)),
            pltpu.SemaphoreType.DMA((SLOTS,)),
        ],
        compiler_params=pltpu.CompilerParams(
            has_side_effects=True, vmem_limit_bytes=60 * 1024 * 1024
        ),
    )(
        window_blocks,
        tok,
        norm_gain.reshape(1, width),
        qk_gain.reshape(2, 4, 128),
        w_spatial.reshape(128, 768),
        w_temporal.reshape(128, 768),
        w_out[:, 0, :],
        w_out[:, 1, :],
    )
    return res.reshape(2, 2, 64, width).transpose(0, 2, 1, 3).reshape(rows, frames, width)


def solution(mesh):
    return jax.shard_map(
        body,
        mesh=mesh,
        in_specs=(
            P("grp", "seq", None),
            P(),
            P(None, None, "grp", None),
            P(),
            P("seq", None, "grp"),
            P("seq", None, "grp"),
            P("seq", None, "grp"),
        ),
        out_specs=P("grp", "seq", None),
        check_vma=False,
    )
```

time: 426 us -> 210 us (0.49)
  waiting for transfers between devices: 286 us -> 0 us
  Pallas kernels: 0 us -> 198 us
  matrix products: 60.8 us -> 0 us
  local copies, waits for them, and re-layouts: 42.2 us -> 9.82 us
  starting transfers between devices: 13.5 us -> 0 us
  between operations: 13.4 us -> 0.04 us
  other arithmetic: 9.69 us -> 0 us
    pallas_call x0 -> x1, Pallas kernels: none -> 198 us  [body(): pl.pallas_call(kernel, name='attention_block', out_shape=jax.ShapeDtypeSt...]
    all_gather x4 -> x0, waiting for transfers between devices: 192 us -> none  [the longest x1 91.2 us: body(): gathered = lax.all_gather(normed, 'grp', axis=0, tiled=True)]
    reduce_scatter x1 -> x0, waiting for transfers between devices: 93.9 us -> none  [body(): lax.psum_scatter(jnp.einsum('pfbc,dbc->pfd', branch_out, full_out, prefer...]
    dot_general x6 -> x0, matrix products: 53.4 us -> none  [the longest x1 15.5 us: spatial_attention(): jnp.einsum('tfhqk,tkfhe->tqfhe', attn_weights, value_tiles, preferred_ele...]
    gather x4 -> x0, local copies, waits for them, and re-layouts: 15.6 us -> none  [the longest x2 7.86 us: spatial_attention(): key_rows.reshape(tile_count, tile_rows, frames, head_count, head_width)]
    all_to_all x2 -> x0, starting transfers between devices: 13.3 us -> none  [the longest x1 7.13 us: body(): lax.all_to_all(packed, 'seq', split_axis=0, concat_axis=1, tiled=True)]
    all_to_all x4 -> x0, local copies, waits for them, and re-layouts: 9.47 us -> none  [the longest x3 8.23 us: body(): lax.all_to_all(packed, 'seq', split_axis=0, concat_axis=1, tiled=True)]
    sub x2 -> x0, matrix products: 7.4 us -> none  [the longest x1 4.98 us: spatial_attention(): scores = jnp.exp(scores - jnp.max(scores, axis=-1, keepdims=True))]
  transfers between devices with their start and end apart: 7 -> 0, of which waited for: 4 -> 0; matrix products, arithmetic and copies ran while one was open for 23% -> 0% of each run, Pallas kernels for 0% -> 0%
where the time goes in v1:
time: 210 us; the launch traced here: 208 us
  Pallas kernels  198 us (94%)
  local copies, waits for them, and re-layouts  9.82 us (5%)
    pallas_call x1, Pallas kernels, body(): pl.pallas_call(kernel, name='attention_block', out_shape=jax.ShapeDtypeSt...  198 us

profile of v1, /device:TPU:1, one launch (start us, length us, event | category | flops | bytes accessed | tf_op | source)
XLA Modules:
  0.0 207.6 jit_solution(6412588682762364748)
XLA Ops:
  0.0 0.0 copy-start.3
  0.0 0.7 copy-done.3
  0.7 0.7 copy.20.win
  1.4 0.0 copy-start.2
  1.4 1.1 copy.16
  2.5 0.0 copy-start
  2.5 0.8 copy.21.w_s
  3.3 0.0 copy-done.2
  3.3 0.2 copy.17
  3.5 0.0 copy-start.1
  3.5 0.8 copy.22.w_t
  4.3 0.1 copy-done.1
  4.4 0.2 fusion
  4.6 0.7 copy_bitcast_fusion
  5.3 0.0 copy-done
  5.3 1.3 copy.15
  6.6 197.7 %attention_block.1 = bf16[256,2048]{1,0:T(8,128)(2,1)} custom-call(s32[8,4]{1,0:T(8,128)} %copy.20.win, bf16[256,2048]{1,0:T(8,128)(2,1)} %bitcast.17, f32[1,2048]{1,0:T(1,128)} %bitcast.21, f32[2,4,128]{2,1,0:T(4,128)} %bitcast.22, bf16[128,768]{1,0:T(8,128)(2,1)} %copy.21.w_s, bf16[128,768]{1,0:T(8,128)(2,1)} %copy.22.w_t, ...), custom_call_target="tpu_custom_call" | custom-call | tf_op jit(solution)/shard_map/attention_block/pallas_call | solution.py:341
  204.3 3.3 %copy.23 = bf16[2,64,2,2048]{3,2,1,0:T(2,128)(2,1)} copy(bf16[2,64,2,2048]{3,1,2,0:T(8,128)(2,1)} %bitcast.16) | data formatting | bytes 2097152 | tf_op jit(solution)/shard_map/transpose | solution.py:375
Async XLA Ops:
  0.0 0.7 copy-start.3
  1.4 2.0 copy-start.2
  2.5 2.8 %copy-start = (bf16[128,2,2048]{2,1,0:T(2,128)(2,1)S(1)}, bf16[128,2,2048]{2,1,0:T(2,128)(2,1)}, u32[]{:S(2)}) copy-start(bf16[128,2,2048]{2,1,0:T(2,128)(2,1)} %param.7) | copy-start | bytes 3145732
  3.5 0.9 copy-start.1

commit v2 on v1

v2 whole, which is shorter than its diff:
```python
import jax
import jax.numpy as jnp
from jax import lax
from jax.experimental import pallas as pl
from jax.experimental.pallas import tpu as pltpu
from jax.sharding import PartitionSpec as P

MESH = pl.DeviceIdType.MESH
EPS = 1e-06
F32 = jnp.float32
BF16 = jnp.bfloat16

TOK, WGT, OUTW, GAIN, RING_TL, RING_TR, RING_W, RING_O, RS, FIN = (
    0, 4, 6, 8, 10, 16, 22, 46, 70, 94,
)
SLOTS = 98


def mm(a, b):
    return jnp.dot(a, b, preferred_element_type=F32)


def mm_t(a, b):
    return lax.dot_general(a, b, (((1,), (1,)), ((), ())), preferred_element_type=F32)


def kernel(
    win, tok, norm_gain, gain, w_s, w_t, wo_s, wo_t, out,
    nrm, xs, wg, wo, gn, qkv, att, part, rs1, rs2, fin, snd, rcv,
):
    s, g = lax.axis_index("seq"), lax.axis_index("grp")
    c, y, xh = lax.rem(s, 2), lax.rem(lax.div(s, 2), 4), lax.div(s, 8)
    xl, z = lax.div(g, 4), lax.rem(g, 4)
    x = xh * 2 + xl
    nc = 1 - c
    unit = c * y + nc * z
    unit2 = nc * y + c * z
    local = nc * xl + c * xh

    def dev(xh_, y_, c_, xl_, z_):
        return ((xh_ * 4 + y_) * 2 + c_, xl_ * 4 + z_)

    def along(dy, dz):
        return dev(xh, lax.rem(y + dy, 4), c, xl, lax.rem(z + dz, 4))

    def across(dx):
        nx = lax.rem(x + dx, 4)
        return dev(lax.div(nx, 2), y, c, lax.rem(nx, 2), z)

    right, left = along(c, nc), along(3 * c, 3 * nc)
    right2, left2 = along(nc, c), along(3 * nc, 3 * c)
    right_x, left_x = across(1), across(3)

    barrier = pltpu.get_barrier_semaphore()
    peers = [right, left, right2, left2, right_x, left_x, dev(xh, y, nc, xl, z)]
    for b in range(2):
        peers.append(dev(xh, y, b, 1 - xl, z))
        peers.append(dev(1 - xh, y, b, xl, z))
        for a in range(2):
            peers.append(dev(xh, z, a, b, y))
    for to in peers:
        pl.semaphore_signal(barrier, inc=1, device_id=to, device_id_type=MESH)

    def remote(src, dst, i, j, to):
        return pltpu.make_async_remote_copy(
            src_ref=src, dst_ref=dst, send_sem=snd.at[i], recv_sem=rcv.at[j],
            device_id=to, device_id_type=MESH,
        )

    sends = []

    def put(src, dst, i, j, to):
        mine = jnp.logical_and(to[0] == s, to[1] == g)
        copy = remote(src, dst, i, j, to)

        @pl.when(mine)
        def _():
            pltpu.make_async_copy(src, dst, rcv.at[j]).start()

        @pl.when(jnp.logical_not(mine))
        def _():
            copy.start()

        sends.append((copy, jnp.logical_not(mine)))

    def arrived(dst, j):
        pltpu.make_async_copy(dst, dst, rcv.at[j]).wait()

    def start(copy):
        copy.start()
        sends.append((copy, None))

    class Ring:
        def __init__(self, view, at, to_right, to_left, base):
            self.view, self.base = view, base
            self.to = (to_right, to_left)
            self.units = (at, lax.rem(at + 3, 4), lax.rem(at + 1, 4), lax.rem(at + 2, 4))

        def send(self, u, half, k, side):
            ref = self.view(self.units[u], half)
            start(remote(ref, ref, self.base + k, self.base + k, self.to[side]))

        def wait(self, *slots):
            for k in slots:
                u, half = ((1, 0), (1, 1), (3, 0), (2, 1), (2, 0), (3, 1))[k]
                arrived(self.view(self.units[u], half), self.base + k)

        def begin(self):
            self.send(0, 0, 0, 0)
            self.send(0, 1, 3, 1)
            self.send(0, 1, 1, 0)
            self.send(0, 0, 4, 1)

        def forward(self):
            self.wait(0)
            self.send(1, 0, 2, 0)
            self.wait(3)
            self.send(2, 1, 5, 1)

    def token_ring(part_, base):
        return Ring(
            lambda u, h: xs.at[u, pl.ds((part_ * 2 + h) * 128, 128)], unit, right, left, base
        )

    def weight_rings(w, base):
        def both(u, h):
            pair = (1 - xl) if h == 0 else xl
            return w.at[pair, :, 1, :, pl.ds(u * 128, 128)]

        return (
            Ring(
                lambda u, h: w.at[xl, xh, 0, :, pl.ds(u * 128 + h * 64, 64)],
                unit2, right2, left2, base,
            ),
            Ring(
                lambda u, h: w.at[lax.rem(u, 2), lax.div(u, 2), 0, :, pl.ds(h * 256, 256)],
                x, right_x, left_x, base + 6,
            ),
            Ring(
                lambda u, h: w.at[
                    lax.rem(u, 2), lax.div(u, 2), 1, :, pl.ds(unit2 * 128 + h * 64, 64)
                ],
                x, right_x, left_x, base + 12,
            ),
            Ring(both, unit2, right2, left2, base + 18),
        )

    tok_l, tok_r = token_ring(local, RING_TL), token_ring(1 - local, RING_TR)
    w1a, w1b, w2a, w2b = weight_rings(wg, RING_W)
    o1a, o1b, o2a, o2b = weight_rings(wo, RING_O)

    def norm_half(h):
        def norm_rows(k, _):
            rows = pl.ds(pl.multiple_of(h * 128 + k * 32, 32), 32)
            v = tok[rows, :].astype(F32)
            scale = lax.rsqrt(jnp.mean(v * v, axis=-1, keepdims=True) + EPS)
            v = (v * scale * norm_gain[...]).astype(BF16)
            for old in range(16):
                new = (old // 8 * 2 + old % 2) * 4 + old // 2 % 4
                nrm[rows, new * 128 : new * 128 + 128] = v[:, old * 128 : old * 128 + 128]
            return 0

        lax.fori_loop(0, 4, norm_rows, 0)

    norm_half(0)
    norm_half(1)
    pl.semaphore_wait(barrier, len(peers))

    to_s, to_t = dev(xh, y, 0, xl, z), dev(xh, z, 1, xl, y)
    mine_w, mine_o = (w.at[xl, xh, c, :, pl.ds(y * 128, 128)] for w in (wg, wo))
    put(w_s, mine_w, WGT, WGT + c, to_s)
    put(w_t, mine_w, WGT + 1, WGT + c, to_t)
    for h in range(2):
        src = nrm.at[pl.ds(h * 128, 128)]
        i_s, i_t = xl * 2 + h, xh * 2 + c
        put(src, xs.at[z, pl.ds(i_s * 128, 128)], TOK + h, TOK + i_s, dev(xh, y, 0, c, z))
        put(src, xs.at[y, pl.ds(i_t * 128, 128)], TOK + 2 + h, TOK + i_t, dev(h, y, 1, xl, z))
    put(wo_s, mine_o, OUTW, OUTW + c, to_s)
    put(wo_t, mine_o, OUTW + 1, OUTW + c, to_t)
    for h in range(2):
        put(
            gain.at[c], gn.at[xl], GAIN + h, GAIN + xl,
            dev(xh, nc * y + c * z, c, h, nc * z + c * y),
        )

    def rows_arrived(w, i, slot):
        arrived(w.at[xl, xh, i, :, pl.ds(unit2 * 128, 128)], slot + i)

    def tokens_arrived(half):
        for h in range(2):
            i = half * 2 + h
            arrived(xs.at[unit, pl.ds(i * 128, 128)], TOK + i)

    rows_arrived(wg, 0, WGT)
    w1a.begin()
    tokens_arrived(local)
    tok_l.begin()
    rows_arrived(wg, 1, WGT)
    w2a.begin()
    w1a.forward()
    w2a.forward()
    w1a.wait(1, 4, 2, 5)
    w1b.begin()
    w2a.wait(1, 4, 2, 5)
    w2b.begin()
    tok_l.forward()
    tokens_arrived(1 - local)
    tok_r.begin()
    w1b.forward()
    w2b.forward()
    tok_r.forward()
    tok_l.wait(1, 4, 2, 5)
    for i in range(2):
        arrived(gn.at[i], GAIN + i)
    tok_r.wait(1, 4, 2, 5)
    w1b.wait(1, 4)
    w2b.wait(1, 4, 2)
    for i in range(2):
        rows_arrived(wo, i, OUTW)
    o1a.begin()
    o2a.begin()

    def project(pair):
        def one(u, _):
            w = [wg[pair, :, :, n].reshape(2048, 256) for n in range(3)]
            acc = mm(xs[u], jnp.concatenate(w, axis=1))
            for n in range(3):
                for j in range(2):
                    a = acc[:, n * 256 + j * 128 : n * 256 + j * 128 + 128]
                    if n < 2:
                        a = a * lax.rsqrt(jnp.mean(a * a, axis=-1, keepdims=True) + EPS)
                        a = a * gn[pair, 2 * n + j : 2 * n + j + 1, :]
                    if n == 0:
                        a = a * (128 ** -0.5)

                    @pl.when(c == 0)
                    def _():
                        b = a.astype(BF16)
                        for k in range(8):
                            i, f = k // 2, k % 2
                            first = f * 64 + ((i // 2) * 4 + u) * 8 + i % 2 * 4
                            qkv[n, pair * 2 + j, pl.ds(first, 4)] = b[
                                k * 64 : k * 64 + 64
                            ].reshape(4, 16, 128)

                    @pl.when(c == 1)
                    def _():
                        for i in range(4):
                            for m in range(8):
                                at = i * 128 + m * 8
                                b = jnp.concatenate([a[at : at + 8], a[at + 64 : at + 72]], axis=0)
                                at = m * 16 + ((i // 2) * 4 + u) * 2 + i % 2
                                qkv[n, pair * 2 + j, at] = b.astype(BF16)
            return 0

        lax.fori_loop(0, 4, one, 0)

    def softmax_mix(sc, v):
        e = jnp.exp(sc - jnp.max(sc, axis=-1, keepdims=True)).astype(BF16)
        o = mm(e, jnp.concatenate([v, jnp.ones_like(v)], axis=1))
        return o[:, 0:128] / o[:, 128:256]

    def tile(n, hd, first, rows=128):
        return qkv[n, hd, pl.ds(first, rows // 16)].reshape(rows, 128)

    def attend(pair, half):
        @pl.when(c == 0)
        def _():
            def spatial(k, _):
                t = half * 4 + k
                for f in range(2):
                    at = [f * 64 + win[j, t] * 8 for j in range(4)]
                    for j in range(2):
                        hd = pair * 2 + j
                        q = tile(0, hd, f * 64 + t * 8)
                        keys = jnp.concatenate([tile(1, hd, a) for a in at], axis=0)
                        vals = jnp.concatenate([tile(2, hd, a) for a in at], axis=0)
                        o = softmax_mix(mm_t(q, keys), vals).astype(BF16)
                        for h in range(2):
                            att[
                                pair, k, half * 4 + h * 2 + f, :, j * 128 : j * 128 + 128
                            ] = o[h * 64 : h * 64 + 64]
                return 0

            lax.fori_loop(0, 4, spatial, 0)

        for b in range(2):
            @pl.when(jnp.logical_and(c == 1, half == b))
            def _():
                def temporal(pg, _):
                    rows = pl.ds(pl.multiple_of(pg * 16, 16), 16)
                    keys = 128 * (b + 1)
                    qi = lax.broadcasted_iota(jnp.int32, (128, keys), 0) + b * 128
                    ki = lax.broadcasted_iota(jnp.int32, (128, keys), 1)
                    ok = jnp.logical_and(
                        jnp.bitwise_and(qi, 7) == jnp.bitwise_and(ki, 7), ki <= qi
                    )
                    for j in range(2):
                        hd = pair * 2 + j
                        res = []
                        for m in range(2):
                            first = pg * 32 + m * 16
                            q = tile(0, hd, first + b * 8)
                            sc = mm_t(q, tile(1, hd, first, keys))
                            res.append(
                                softmax_mix(jnp.where(ok, sc, -1e30), tile(2, hd, first, keys))
                            )
                        for m in range(16):
                            fr = b * 16 + m
                            i = b * 2 + (fr // 2) % 2
                            o = jnp.concatenate([v[m * 8 : m * 8 + 8] for v in res], axis=0)
                            att[
                                pair, fr // 4 % 4, i * 2 + fr % 2, rows, j * 128 : j * 128 + 128
                            ] = o.astype(BF16)
                    return 0

                lax.fori_loop(0, 4, temporal, 0)

    project(1 - xl)
    o1a.forward()
    o2a.forward()
    attend(1 - xl, 0)
    o1a.wait(1, 4, 2, 5)
    o1b.begin()
    o2a.wait(1, 4, 2, 5)
    o2b.begin()
    attend(1 - xl, 1)
    w1b.wait(2, 5)
    w2b.wait(5)
    o1b.forward()
    o2b.forward()
    project(xl)
    attend(xl, 1 - local)
    o1b.wait(1, 4, 2, 5)
    o2b.wait(1, 4, 2, 5)

    def outproj(u, half):
        def one(k, _):
            rows = pl.ds(pl.multiple_of(half * 256, 256), 256)
            o = [att[p, u, pl.ds(half * 4, 4)].reshape(256, 256) for p in range(2)]
            for b in range(2):
                acc = mm_t(o[0], wo[0, k, b, 0]) + mm_t(o[1], wo[1, k, b, 0])
                for q in range(4):
                    cols = pl.ds(pl.multiple_of(k * 1024 + q * 256 + b * 128, 128), 128)
                    part[u, rows, cols] = acc[:, q * 128 : q * 128 + 128].astype(BF16)
            return 0

        lax.fori_loop(0, 2, one, 0)

    def add_rows(u, first, *others):
        def one(k, _):
            rows = pl.ds(pl.multiple_of(first + k * 32, 32), 32)
            here = pl.ds(pl.multiple_of(k * 32, 32), 32)
            total = part[u, rows, :].astype(F32)
            for other in others:
                total = total + other[here, :].astype(F32)
            part[u, rows, :] = total.astype(BF16)
            return 0

        lax.fori_loop(0, 2, one, 0)

    u_l, u_r, u_2 = lax.rem(unit + 3, 4), lax.rem(unit + 1, 4), lax.rem(unit + 2, 4)
    pieces = [(1 - local) * 2, (1 - local) * 2 + 1, local * 2, local * 2 + 1]

    def reduce_send(n, u, q, dst, k, to):
        src = part.at[u, pl.ds(pieces[n] * 128 + q * 64, 64)]
        start(remote(src, dst, RS + n * 6 + k, RS + n * 6 + k, to))

    def reduce_start(half, n):
        outproj(u_2, half)
        reduce_send(n, u_2, 0, rs1.at[n, 0], 0, right)
        reduce_send(n, u_2, 1, rs1.at[n, 1], 1, left)
        outproj(u_r, half)
        reduce_send(n, u_r, 1, rs2.at[n, 0, 1], 2, right)
        outproj(u_l, half)
        reduce_send(n, u_l, 0, rs2.at[n, 1, 0], 3, left)
        reduce_send(n + 1, u_2, 0, rs1.at[n + 1, 0], 0, right)
        reduce_send(n + 1, u_2, 1, rs1.at[n + 1, 1], 1, left)
        reduce_send(n + 1, u_r, 1, rs2.at[n + 1, 0, 1], 2, right)
        reduce_send(n + 1, u_l, 0, rs2.at[n + 1, 1, 0], 3, left)

    def reduce_pass(n):
        arrived(rs1.at[n, 0], RS + n * 6)
        add_rows(u_r, pieces[n] * 128, rs1.at[n, 0])
        reduce_send(n, u_r, 0, rs2.at[n, 0, 0], 4, right)
        arrived(rs1.at[n, 1], RS + n * 6 + 1)
        add_rows(u_l, pieces[n] * 128 + 64, rs1.at[n, 1])
        reduce_send(n, u_l, 1, rs2.at[n, 1, 1], 5, left)

    def reduce_end(half, n):
        h = n % 2
        for q in range(2):
            arrived(rs2.at[n, 1 - q, q], RS + n * 6 + 3 - q)
            arrived(rs2.at[n, q, q], RS + n * 6 + 4 + q)
            add_rows(unit, pieces[n] * 128 + q * 64, rs2.at[n, 0, q], rs2.at[n, 1, q])
        at = nc * h + c * (2 + xh)
        to = dev(nc * xh + c * half, y, nc * xl + c * h, nc * half + c * xl, z)
        put(part.at[unit, pl.ds(pieces[n] * 128, 128)], fin.at[at], FIN + n, FIN + at, to)

    reduce_start(1 - local, 0)
    attend(xl, local)
    reduce_pass(0)
    reduce_pass(1)
    outproj(unit, 1 - local)
    reduce_start(local, 2)
    reduce_end(1 - local, 0)
    reduce_end(1 - local, 1)
    reduce_pass(2)
    reduce_pass(3)
    outproj(unit, local)
    reduce_end(local, 2)
    reduce_end(local, 3)

    for h in range(2):
        arrived(fin.at[h], FIN + h)
        arrived(fin.at[2 + h], FIN + 2 + h)

        def total_rows(k, _):
            rows = pl.ds(pl.multiple_of(k * 32, 32), 32)
            here = pl.ds(pl.multiple_of(h * 128 + k * 32, 32), 32)
            total = fin[h, rows, :].astype(F32) + fin[2 + h, rows, :].astype(F32)
            out[here, :] = (tok[here, :].astype(F32) + total).astype(BF16)
            return 0

        lax.fori_loop(0, 4, total_rows, 0)

    for copy, cond in sends:
        if cond is None:
            copy.wait_send()
        else:
            pl.when(cond)(copy.wait_send)


def body(tokens, norm_gain, qk_gain, window_blocks, w_spatial, w_temporal, w_out):
    rows, frames, width = tokens.shape
    tok = tokens.reshape(2, 64, 2, width).transpose(0, 2, 1, 3).reshape(256, width)
    vmem = pl.BlockSpec(memory_space=pltpu.VMEM)
    res = pl.pallas_call(
        kernel,
        name="attention_block",
        out_shape=jax.ShapeDtypeStruct((256, width), BF16),
        in_specs=[pl.BlockSpec(memory_space=pltpu.SMEM)] + [vmem] * 7,
        out_specs=vmem,
        scratch_shapes=[
            pltpu.VMEM((256, 2048), BF16),
            pltpu.VMEM((4, 512, 2048), BF16),
            pltpu.VMEM((2, 2, 2, 3, 512, 256), BF16),
            pltpu.VMEM((2, 2, 2, 1, 512, 256), BF16),
            pltpu.VMEM((2, 4, 128), F32),
            pltpu.VMEM((3, 4, 128, 16, 128), BF16),
            pltpu.VMEM((2, 4, 8, 64, 256), BF16),
            pltpu.VMEM((4, 512, 2048), BF16),
            pltpu.VMEM((4, 2, 64, 2048), BF16),
            pltpu.VMEM((4, 2, 2, 64, 2048), BF16),
            pltpu.VMEM((4, 128, 2048), BF16),
            pltpu.SemaphoreType.DMA((SLOTS,)),
            pltpu.SemaphoreType.DMA((SLOTS,)),
        ],
        compiler_params=pltpu.CompilerParams(
            collective_id=0, has_side_effects=True, vmem_limit_bytes=60 * 1024 * 1024
        ),
    )(
        window_blocks.T,
        tok,
        norm_gain.reshape(1, width),
        qk_gain.reshape(2, 4, 128),
        w_spatial.transpose(1, 0, 2),
        w_temporal.transpose(1, 0, 2),
        w_out[:, 0, :].reshape(1, 128, 256),
        w_out[:, 1, :].reshape(1, 128, 256),
    )
    return res.reshape(2, 2, 64, width).transpose(0, 2, 1, 3).reshape(rows, frames, width)


def solution(mesh):
    return jax.shard_map(
        body,
        mesh=mesh,
        in_specs=(
            P("grp", "seq", None),
            P(),
            P(None, None, "grp", None),
            P(),
            P("seq", None, "grp"),
            P("seq", None, "grp"),
            P("seq", None, "grp"),
        ),
        out_specs=P("grp", "seq", None),
        check_vma=False,
    )
```

time: 210 us -> 164 us (0.78); the launches traced: 208 us -> 164 us
  Pallas kernels: 198 us -> 156 us
  local copies, waits for them, and re-layouts: 9.82 us -> 7.69 us
    pallas_call x1, Pallas kernels: 198 us -> 156 us  [body(): pl.pallas_call(kernel, name='attention_block', out_shape=jax.ShapeDtypeSt...]
    unnamed x11 -> x0, local copies, waits for them, and re-layouts: 2.71 us -> none
where the time goes in v2:
time: 164 us
  Pallas kernels  156 us (95%)
  local copies, waits for them, and re-layouts  7.69 us (5%)
    pallas_call x1, Pallas kernels, body(): pl.pallas_call(kernel, name='attention_block', out_shape=jax.ShapeDtypeSt...  156 us

profile of v2, /device:TPU:1, one launch (start us, length us, event | category | flops | bytes accessed | tf_op | source)
XLA Modules:
  0.0 164.2 jit_solution(528943526201268692)
XLA Ops:
  0.0 1.2 fusion
  1.2 0.7 copy_bitcast_fusion
  1.9 2.5 %copy.8 = bf16[2,64,2,2048]{3,1,2,0:T(8,128)(2,1)} copy(bf16[2,64,2,2048]{3,2,1,0:T(2,128)(2,1)} %bitcast.19) | data formatting | bytes 2097152 | tf_op jit(solution)/shard_map/reshape | solution.py:436
  4.4 156.5 %attention_block.1 = bf16[256,2048]{1,0:T(8,128)(2,1)} custom-call(s32[4,8]{1,0:T(4,128)} %bitcast.24, bf16[256,2048]{1,0:T(8,128)(2,1)} %bitcast.18, f32[1,2048]{1,0:T(1,128)} %bitcast.22, f32[2,4,128]{2,1,0:T(4,128)} %bitcast.23, bf16[3,128,256]{2,1,0:T(8,128)(2,1)} %bitcast.20, bf16[3,128,256]{2,1,0:T(8,128)(2,1)} %bitcast.21, ...), custom_call_target="tpu_custom_call" | custom-call | tf_op jit(solution)/shard_map/attention_block/pallas_call | solution.py:438
  160.9 3.3 %copy.11 = bf16[2,64,2,2048]{3,2,1,0:T(2,128)(2,1)} copy(bf16[2,64,2,2048]{3,1,2,0:T(8,128)(2,1)} %bitcast.17) | data formatting | bytes 2097152 | tf_op jit(solution)/shard_map/transpose | solution.py:472

commit v3 on v2

--- a/solution.py
+++ b/solution.py
@@ -11,9 +11,9 @@
 BF16 = jnp.bfloat16
 
 TOK, WGT, OUTW, GAIN, RING_TL, RING_TR, RING_W, RING_O, RS, FIN = (
-    0, 4, 6, 8, 10, 16, 22, 46, 70, 94,
+    0, 4, 6, 8, 10, 16, 22, 52, 82, 106,
 )
-SLOTS = 98
+SLOTS = 110
 
 
 def mm(a, b):
@@ -117,16 +117,25 @@
             self.wait(3)
             self.send(2, 1, 5, 1)
 
+        def forward_x(self):
+            unit_ = (1 - xl) * self.units[2] + xl * self.units[1]
+            to = tuple((1 - xl) * b + xl * a for a, b in zip(*self.to))
+            for half, slot in ((0, 4 * (1 - xl)), (1, 3 - 2 * xl)):
+                ref, k = self.view(unit_, half), self.base + 2 + 3 * half
+                arrived(ref, self.base + slot)
+                start(remote(ref, ref, k, k, to))
+
+        def near_x(self):
+            unit_ = (1 - xl) * self.units[1] + xl * self.units[2]
+            for half, slot in ((0, 4 * xl), (1, 1 + 2 * xl)):
+                arrived(self.view(unit_, half), self.base + slot)
+
     def token_ring(part_, base):
         return Ring(
             lambda u, h: xs.at[u, pl.ds((part_ * 2 + h) * 128, 128)], unit, right, left, base
         )
 
     def weight_rings(w, base):
-        def both(u, h):
-            pair = (1 - xl) if h == 0 else xl
-            return w.at[pair, :, 1, :, pl.ds(u * 128, 128)]
-
         return (
             Ring(
                 lambda u, h: w.at[xl, xh, 0, :, pl.ds(u * 128 + h * 64, 64)],
@@ -142,12 +151,19 @@
                 ],
                 x, right_x, left_x, base + 12,
             ),
-            Ring(both, unit2, right2, left2, base + 18),
+            Ring(
+                lambda u, h: w.at[1 - xl, h, 1, :, pl.ds(u * 128, 128)],
+                unit2, right2, left2, base + 18,
+            ),
+            Ring(
+                lambda u, h: w.at[xl, h, 1, :, pl.ds(u * 128, 128)],
+                unit2, right2, left2, base + 24,
+            ),
         )
 
     tok_l, tok_r = token_ring(local, RING_TL), token_ring(1 - local, RING_TR)
-    w1a, w1b, w2a, w2b = weight_rings(wg, RING_W)
-    o1a, o1b, o2a, o2b = weight_rings(wo, RING_O)
+    w1a, w1b, w2a, w2b, w2c = weight_rings(wg, RING_W)
+    o1a, o1b, o2a, o2b, o2c = weight_rings(wo, RING_O)
 
     def norm_half(h):
         def norm_rows(k, _):
@@ -191,36 +207,39 @@
             i = half * 2 + h
             arrived(xs.at[unit, pl.ds(i * 128, 128)], TOK + i)
 
+    tokens_arrived(local)
+    tok_l.begin()
     rows_arrived(wg, 0, WGT)
     w1a.begin()
-    tokens_arrived(local)
-    tok_l.begin()
     rows_arrived(wg, 1, WGT)
     w2a.begin()
+    tok_l.forward()
     w1a.forward()
+    tokens_arrived(1 - local)
+    tok_r.begin()
     w2a.forward()
+    for i in range(2):
+        rows_arrived(wo, i, OUTW)
+    o1a.begin()
+    o2a.begin()
     w1a.wait(1, 4, 2, 5)
     w1b.begin()
     w2a.wait(1, 4, 2, 5)
     w2b.begin()
-    tok_l.forward()
-    tokens_arrived(1 - local)
-    tok_r.begin()
-    w1b.forward()
+    tok_r.forward()
+    o1a.forward()
+    o2a.forward()
     w2b.forward()
-    tok_r.forward()
+    w1b.forward_x()
+    w2c.begin()
     tok_l.wait(1, 4, 2, 5)
     for i in range(2):
         arrived(gn.at[i], GAIN + i)
     tok_r.wait(1, 4, 2, 5)
-    w1b.wait(1, 4)
-    w2b.wait(1, 4, 2)
-    for i in range(2):
-        rows_arrived(wo, i, OUTW)
-    o1a.begin()
-    o2a.begin()
-
-    def project(pair):
+    w1b.near_x()
+    w2b.wait(1, 4, 2, 5)
+
+    def project(pair, first, last):
         def one(u, _):
             w = [wg[pair, :, :, n].reshape(2048, 256) for n in range(3)]
             acc = mm(xs[u], jnp.concatenate(w, axis=1))
@@ -253,7 +272,7 @@
                                 qkv[n, pair * 2 + j, at] = b.astype(BF16)
             return 0
 
-        lax.fori_loop(0, 4, one, 0)
+        lax.fori_loop(first, last, one, 0)
 
     def softmax_mix(sc, v):
         e = jnp.exp(sc - jnp.max(sc, axis=-1, keepdims=True)).astype(BF16)
@@ -316,23 +335,28 @@
 
                 lax.fori_loop(0, 4, temporal, 0)
 
-    project(1 - xl)
-    o1a.forward()
-    o2a.forward()
-    attend(1 - xl, 0)
+    project(1 - xl, 0, 2)
+    w2c.forward()
     o1a.wait(1, 4, 2, 5)
     o1b.begin()
     o2a.wait(1, 4, 2, 5)
     o2b.begin()
+    o2c.begin()
+    project(1 - xl, 2, 4)
+    attend(1 - xl, 0)
+    o1b.forward_x()
+    o2b.forward()
+    o2c.forward()
     attend(1 - xl, 1)
     w1b.wait(2, 5)
-    w2b.wait(5)
-    o1b.forward()
-    o2b.forward()
-    project(xl)
+    w2c.wait(1, 4, 2, 5)
+    project(xl, 0, 2)
+    project(xl, 2, 4)
     attend(xl, 1 - local)
-    o1b.wait(1, 4, 2, 5)
+    o1b.near_x()
+    o1b.wait(2, 5)
     o2b.wait(1, 4, 2, 5)
+    o2c.wait(1, 4, 2, 5)
 
     def outproj(u, half):
         def one(k, _):

time: 164 us -> 152 us (0.927); the launches traced: 164 us -> 151 us
  Pallas kernels: 156 us -> 143 us
    pallas_call x1, Pallas kernels: 156 us -> 143 us  [body(): pl.pallas_call(kernel, name='attention_block', out_shape=jax.ShapeDtypeSt...]
where the time goes in v3:
time: 152 us; the launch traced here: 151 us
  Pallas kernels  143 us (94%)
  local copies, waits for them, and re-layouts  7.69 us (5%)
    pallas_call x1, Pallas kernels, body(): pl.pallas_call(kernel, name='attention_block', out_shape=jax.ShapeDtypeSt...  143 us
    transpose x1, local copies, waits for them, and re-layouts, body(): res.reshape(2, 2, 64, width).transpose(0, 2, 1, 3)  3.27 us

profile of v3, /device:TPU:1, one launch (start us, length us, event | category | flops | bytes accessed | tf_op | source)
XLA Modules:
  0.0 150.5 jit_solution(13162252849846962667)
XLA Ops:
  0.0 1.2 fusion
  1.2 0.7 copy_bitcast_fusion
  1.9 2.5 %copy.8 = bf16[2,64,2,2048]{3,1,2,0:T(8,128)(2,1)} copy(bf16[2,64,2,2048]{3,2,1,0:T(2,128)(2,1)} %bitcast.19) | data formatting | bytes 2097152 | tf_op jit(solution)/shard_map/reshape | solution.py:460
  4.4 142.8 %attention_block.1 = bf16[256,2048]{1,0:T(8,128)(2,1)} custom-call(s32[4,8]{1,0:T(4,128)} %bitcast.24, bf16[256,2048]{1,0:T(8,128)(2,1)} %bitcast.18, f32[1,2048]{1,0:T(1,128)} %bitcast.22, f32[2,4,128]{2,1,0:T(4,128)} %bitcast.23, bf16[3,128,256]{2,1,0:T(8,128)(2,1)} %bitcast.20, bf16[3,128,256]{2,1,0:T(8,128)(2,1)} %bitcast.21, ...), custom_call_target="tpu_custom_call" | custom-call | tf_op jit(solution)/shard_map/attention_block/pallas_call | solution.py:462
  147.2 3.3 %copy.11 = bf16[2,64,2,2048]{3,2,1,0:T(2,128)(2,1)} copy(bf16[2,64,2,2048]{3,1,2,0:T(8,128)(2,1)} %bitcast.17) | data formatting | bytes 2097152 | tf_op jit(solution)/shard_map/transpose | solution.py:496

commit v4 on v3

--- a/solution.py
+++ b/solution.py
@@ -25,8 +25,8 @@
 
 
 def kernel(
-    win, tok, norm_gain, gain, w_s, w_t, wo_s, wo_t, out,
-    nrm, xs, wg, wo, gn, qkv, att, part, rs1, rs2, fin, snd, rcv,
+    win, tok, norm_gain, gain, w_s, w_t, w_o, out,
+    nrm, wo_own, xs, wg, wo, gn, qkv, att, part, rs1, rs2, fin, snd, rcv,
 ):
     s, g = lax.axis_index("seq"), lax.axis_index("grp")
     c, y, xh = lax.rem(s, 2), lax.rem(lax.div(s, 2), 4), lax.div(s, 8)
@@ -191,8 +191,10 @@
         i_s, i_t = xl * 2 + h, xh * 2 + c
         put(src, xs.at[z, pl.ds(i_s * 128, 128)], TOK + h, TOK + i_s, dev(xh, y, 0, c, z))
         put(src, xs.at[y, pl.ds(i_t * 128, 128)], TOK + 2 + h, TOK + i_t, dev(h, y, 1, xl, z))
-    put(wo_s, mine_o, OUTW, OUTW + c, to_s)
-    put(wo_t, mine_o, OUTW + 1, OUTW + c, to_t)
+    for b in range(2):
+        wo_own[b, 0] = w_o[...].astype(F32)[:, b, :].astype(BF16)
+    put(wo_own.at[0], mine_o, OUTW, OUTW + c, to_s)
+    put(wo_own.at[1], mine_o, OUTW + 1, OUTW + c, to_t)
     for h in range(2):
         put(
             gain.at[c], gn.at[xl], GAIN + h, GAIN + xl,
@@ -462,11 +464,12 @@
     res = pl.pallas_call(
         kernel,
         name="attention_block",
-        out_shape=jax.ShapeDtypeStruct((256, width), BF16),
-        in_specs=[pl.BlockSpec(memory_space=pltpu.SMEM)] + [vmem] * 7,
+        out_shape=pltpu.VMEM((256, width), BF16),
+        in_specs=[pl.BlockSpec(memory_space=pltpu.SMEM)] + [vmem] * 6,
         out_specs=vmem,
         scratch_shapes=[
             pltpu.VMEM((256, 2048), BF16),
+            pltpu.VMEM((2, 1, 128, 256), BF16),
             pltpu.VMEM((4, 512, 2048), BF16),
             pltpu.VMEM((2, 2, 2, 3, 512, 256), BF16),
             pltpu.VMEM((2, 2, 2, 1, 512, 256), BF16),
@@ -485,13 +488,12 @@
         ),
     )(
         window_blocks.T,
-        tok,
+        pltpu.with_memory_space_constraint(tok, pltpu.VMEM),
         norm_gain.reshape(1, width),
         qk_gain.reshape(2, 4, 128),
         w_spatial.transpose(1, 0, 2),
         w_temporal.transpose(1, 0, 2),
-        w_out[:, 0, :].reshape(1, 128, 256),
-        w_out[:, 1, :].reshape(1, 128, 256),
+        w_out,
     )
     return res.reshape(2, 2, 64, width).transpose(0, 2, 1, 3).reshape(rows, frames, width)
 

time: 152 us -> 147 us (0.967)
  local copies, waits for them, and re-layouts: 7.69 us -> 3.62 us
where the time goes in v4:
time: 147 us; the launch traced here: 145 us
  Pallas kernels  142 us (97%)
  local copies, waits for them, and re-layouts  3.62 us (2%)
    pallas_call x1, Pallas kernels, body(): pl.pallas_call(kernel, name='attention_block', out_shape=pltpu.VMEM((256,...  142 us

profile of v4, /device:TPU:1, one launch (start us, length us, event | category | flops | bytes accessed | tf_op | source)
XLA Modules:
  0.0 145.3 jit_solution(15056840255126563388)
XLA Ops:
  0.0 1.6 %copy.8 = bf16[2,64,2,2048]{3,1,2,0:T(8,128)(2,1)S(1)} copy(bf16[2,64,2,2048]{3,2,1,0:T(2,128)(2,1)} %bitcast.15) | data formatting | bytes 2097152 | tf_op jit(solution)/shard_map/reshape | solution.py:462
  1.6 141.6 %attention_block.1 = bf16[256,2048]{1,0:T(8,128)(2,1)S(1)} custom-call(s32[4,8]{1,0:T(4,128)} %bitcast.20, bf16[256,2048]{1,0:T(8,128)(2,1)S(1)} %bitcast.14, f32[1,2048]{1,0:T(1,128)} %bitcast.18, f32[2,4,128]{2,1,0:T(4,128)} %bitcast.19, bf16[3,128,256]{2,1,0:T(8,128)(2,1)} %bitcast.16, bf16[3,128,256]{2,1,0:T(8,128)(2,1)} %bitcast.17, ...), custom_call_target="tpu_custom_call" | custom-call | tf_op jit(solution)/shard_map/attention_block/pallas_call | solution.py:464
  143.2 2.0 %copy.9 = bf16[2,64,2,2048]{3,2,1,0:T(2,128)(2,1)} copy(bf16[2,64,2,2048]{3,1,2,0:T(8,128)(2,1)S(1)} %bitcast.13) | data formatting | bytes 2097152 | tf_op jit(solution)/shard_map/transpose | solution.py:498

commit v5 on v4

--- a/solution.py
+++ b/solution.py
@@ -242,7 +242,7 @@
     w2b.wait(1, 4, 2, 5)
 
     def project(pair, first, last):
-        def one(u, _):
+        def one(role, u, _):
             w = [wg[pair, :, :, n].reshape(2048, 256) for n in range(3)]
             acc = mm(xs[u], jnp.concatenate(w, axis=1))
             for n in range(3):
@@ -254,18 +254,15 @@
                     if n == 0:
                         a = a * (128 ** -0.5)
 
-                    @pl.when(c == 0)
-                    def _():
+                    if role == 0:
                         b = a.astype(BF16)
                         for k in range(8):
                             i, f = k // 2, k % 2
-                            first = f * 64 + ((i // 2) * 4 + u) * 8 + i % 2 * 4
-                            qkv[n, pair * 2 + j, pl.ds(first, 4)] = b[
+                            at = f * 64 + ((i // 2) * 4 + u) * 8 + i % 2 * 4
+                            qkv[n, pair * 2 + j, pl.ds(at, 4)] = b[
                                 k * 64 : k * 64 + 64
                             ].reshape(4, 16, 128)
-
-                    @pl.when(c == 1)
-                    def _():
+                    else:
                         for i in range(4):
                             for m in range(8):
                                 at = i * 128 + m * 8
@@ -274,7 +271,10 @@
                                 qkv[n, pair * 2 + j, at] = b.astype(BF16)
             return 0
 
-        lax.fori_loop(first, last, one, 0)
+        for role in range(2):
+            @pl.when(c == role)
+            def _():
+                lax.fori_loop(first, last, lambda u, v: one(role, u, v), 0)
 
     def softmax_mix(sc, v):
         e = jnp.exp(sc - jnp.max(sc, axis=-1, keepdims=True)).astype(BF16)

time: 147 us -> 144 us (0.980)
  Pallas kernels: 142 us -> 138 us
    pallas_call x1, Pallas kernels: 142 us -> 138 us  [body(): pl.pallas_call(kernel, name='attention_block', out_shape=pltpu.VMEM((256,...]
where the time goes in v5:
time: 144 us; the launch traced here: 142 us
  Pallas kernels  138 us (96%)
  local copies, waits for them, and re-layouts  3.62 us (3%)
    pallas_call x1, Pallas kernels, body(): pl.pallas_call(kernel, name='attention_block', out_shape=pltpu.VMEM((256,...  138 us

profile of v5, /device:TPU:1, one launch (start us, length us, event | category | flops | bytes accessed | tf_op | source)
XLA Modules:
  0.0 141.8 jit_solution(17548080792888067186)
XLA Ops:
  0.0 1.6 %copy.8 = bf16[2,64,2,2048]{3,1,2,0:T(8,128)(2,1)S(1)} copy(bf16[2,64,2,2048]{3,2,1,0:T(2,128)(2,1)} %bitcast.15) | data formatting | bytes 2097152 | tf_op jit(solution)/shard_map/reshape | solution.py:462
  1.6 138.1 %attention_block.1 = bf16[256,2048]{1,0:T(8,128)(2,1)S(1)} custom-call(s32[4,8]{1,0:T(4,128)} %bitcast.20, bf16[256,2048]{1,0:T(8,128)(2,1)S(1)} %bitcast.14, f32[1,2048]{1,0:T(1,128)} %bitcast.18, f32[2,4,128]{2,1,0:T(4,128)} %bitcast.19, bf16[3,128,256]{2,1,0:T(8,128)(2,1)} %bitcast.16, bf16[3,128,256]{2,1,0:T(8,128)(2,1)} %bitcast.17, ...), custom_call_target="tpu_custom_call" | custom-call | tf_op jit(solution)/shard_map/attention_block/pallas_call | solution.py:464
  139.7 2.0 %copy.9 = bf16[2,64,2,2048]{3,2,1,0:T(2,128)(2,1)} copy(bf16[2,64,2,2048]{3,1,2,0:T(8,128)(2,1)S(1)} %bitcast.13) | data formatting | bytes 2097152 | tf_op jit(solution)/shard_map/transpose | solution.py:498

commit v6 on v5

--- a/solution.py
+++ b/solution.py
@@ -303,7 +303,7 @@
                             ] = o[h * 64 : h * 64 + 64]
                 return 0
 
-            lax.fori_loop(0, 4, spatial, 0)
+            lax.fori_loop(0, 4, spatial, 0, unroll=2)
 
         for b in range(2):
             @pl.when(jnp.logical_and(c == 1, half == b))
@@ -335,7 +335,7 @@
                             ] = o.astype(BF16)
                     return 0
 
-                lax.fori_loop(0, 4, temporal, 0)
+                lax.fori_loop(0, 4, temporal, 0, unroll=2)
 
     project(1 - xl, 0, 2)
     w2c.forward()

time: 144 us -> 142 us (0.986)
    pallas_call x1, Pallas kernels: 138 us -> 137 us  [body(): pl.pallas_call(kernel, name='attention_block', out_shape=pltpu.VMEM((256,...]
where the time goes in v6:
time: 142 us; the launch traced here: 140 us
  Pallas kernels  137 us (96%)
  local copies, waits for them, and re-layouts  3.62 us (3%)
    pallas_call x1, Pallas kernels, body(): pl.pallas_call(kernel, name='attention_block', out_shape=pltpu.VMEM((256,...  137 us

profile of v6, /device:TPU:1, one launch (start us, length us, event | category | flops | bytes accessed | tf_op | source)
XLA Modules:
  0.0 140.2 jit_solution(2307836900663035232)
XLA Ops:
  0.0 1.6 %copy.8 = bf16[2,64,2,2048]{3,1,2,0:T(8,128)(2,1)S(1)} copy(bf16[2,64,2,2048]{3,2,1,0:T(2,128)(2,1)} %bitcast.15) | data formatting | bytes 2097152 | tf_op jit(solution)/shard_map/reshape | solution.py:462
  1.6 136.6 %attention_block.1 = bf16[256,2048]{1,0:T(8,128)(2,1)S(1)} custom-call(s32[4,8]{1,0:T(4,128)} %bitcast.20, bf16[256,2048]{1,0:T(8,128)(2,1)S(1)} %bitcast.14, f32[1,2048]{1,0:T(1,128)} %bitcast.18, f32[2,4,128]{2,1,0:T(4,128)} %bitcast.19, bf16[3,128,256]{2,1,0:T(8,128)(2,1)} %bitcast.16, bf16[3,128,256]{2,1,0:T(8,128)(2,1)} %bitcast.17, ...), custom_call_target="tpu_custom_call" | custom-call | tf_op jit(solution)/shard_map/attention_block/pallas_call | solution.py:464
  138.2 2.0 %copy.9 = bf16[2,64,2,2048]{3,2,1,0:T(2,128)(2,1)} copy(bf16[2,64,2,2048]{3,1,2,0:T(8,128)(2,1)S(1)} %bitcast.13) | data formatting | bytes 2097152 | tf_op jit(solution)/shard_map/transpose | solution.py:498

commit v7 on v6

--- a/solution.py
+++ b/solution.py
@@ -284,10 +284,11 @@
     def tile(n, hd, first, rows=128):
         return qkv[n, hd, pl.ds(first, rows // 16)].reshape(rows, 128)
 
-    def attend(pair, half):
+    def attend(pair, half, first=0, last=4):
         @pl.when(c == 0)
         def _():
             def spatial(k, _):
+                k = lax.rem(unit + 2 + k, 4)
                 t = half * 4 + k
                 for f in range(2):
                     at = [f * 64 + win[j, t] * 8 for j in range(4)]
@@ -303,9 +304,9 @@
                             ] = o[h * 64 : h * 64 + 64]
                 return 0
 
-            lax.fori_loop(0, 4, spatial, 0, unroll=2)
-
-        for b in range(2):
+            lax.fori_loop(first, last, spatial, 0, unroll=2 if last - first == 4 else last - first)
+
+        for b in range(2 if first == 0 else 0):
             @pl.when(jnp.logical_and(c == 1, half == b))
             def _():
                 def temporal(pg, _):
@@ -354,7 +355,7 @@
     w2c.wait(1, 4, 2, 5)
     project(xl, 0, 2)
     project(xl, 2, 4)
-    attend(xl, 1 - local)
+    attend(xl, 1 - local, 0, 1)
     o1b.near_x()
     o1b.wait(2, 5)
     o2b.wait(1, 4, 2, 5)
@@ -396,6 +397,8 @@
         outproj(u_2, half)
         reduce_send(n, u_2, 0, rs1.at[n, 0], 0, right)
         reduce_send(n, u_2, 1, rs1.at[n, 1], 1, left)
+        if n == 0:
+            attend(xl, half, 1, 4)
         outproj(u_r, half)
         reduce_send(n, u_r, 1, rs2.at[n, 0, 1], 2, right)
         outproj(u_l, half)

time: 142 us -> 141 us (level)
  no operation moved by 1% of the time
where the time goes in v7:
time: 141 us; the launch traced here: 140 us
  Pallas kernels  136 us (96%)
  local copies, waits for them, and re-layouts  3.62 us (3%)
    pallas_call x1, Pallas kernels, body(): pl.pallas_call(kernel, name='attention_block', out_shape=pltpu.VMEM((256,...  136 us

profile of v7, /device:TPU:1, one launch (start us, length us, event | category | flops | bytes accessed | tf_op | source)
XLA Modules:
  0.0 139.7 jit_solution(614486061302918243)
XLA Ops:
  0.0 1.6 %copy.8 = bf16[2,64,2,2048]{3,1,2,0:T(8,128)(2,1)S(1)} copy(bf16[2,64,2,2048]{3,2,1,0:T(2,128)(2,1)} %bitcast.15) | data formatting | bytes 2097152 | tf_op jit(solution)/shard_map/reshape | solution.py:465
  1.6 136.1 %attention_block.1 = bf16[256,2048]{1,0:T(8,128)(2,1)S(1)} custom-call(s32[4,8]{1,0:T(4,128)} %bitcast.20, bf16[256,2048]{1,0:T(8,128)(2,1)S(1)} %bitcast.14, f32[1,2048]{1,0:T(1,128)} %bitcast.18, f32[2,4,128]{2,1,0:T(4,128)} %bitcast.19, bf16[3,128,256]{2,1,0:T(8,128)(2,1)} %bitcast.16, bf16[3,128,256]{2,1,0:T(8,128)(2,1)} %bitcast.17, ...), custom_call_target="tpu_custom_call" | custom-call | tf_op jit(solution)/shard_map/attention_block/pallas_call | solution.py:467
  137.7 2.0 %copy.9 = bf16[2,64,2,2048]{3,2,1,0:T(2,128)(2,1)} copy(bf16[2,64,2,2048]{3,1,2,0:T(8,128)(2,1)S(1)} %bitcast.13) | data formatting | bytes 2097152 | tf_op jit(solution)/shard_map/transpose | solution.py:501
